TPU v7x, 32 devices: a whole 2x2x4 slice. The times are simulated.
32 devices in a mesh: clip: 2 (over x), blk: 16 (over z, y, core).
Axes of the slice: x: 2, y: 2, z: 4, core: 2. Of those that a mesh axis runs over, the one named last changes fastest.
Arguments:
- queries: bfloat16 [8192, 2560], P(('clip', 'blk')), parts along dimension 0, may hold values from -24 to 24
- keys: bfloat16 [8192, 2560], P(('clip', 'blk')), parts along dimension 0, may hold values from -24 to 24
- values: bfloat16 [8192, 2560], P(('clip', 'blk')), parts along dimension 0, may hold values from -6 to 6
- kept_blocks: int32 [64, 8], P(('clip', 'blk')), parts along dimension 0, may hold values from 0 to 31, as said below
Outputs:
- attended: bfloat16 [8192, 2560], P(('clip', 'blk')), parts along dimension 0
There are 2 independent parts, one for each index of `clip`. A program takes and returns all parts, laid end to end along the dimension named above; each array names one. Nothing has to cross between parts.
Inputs may be any that keep to these rules, and one draw needn't show every extreme that they name: `kept_blocks`: row b lists 8 distinct key blocks in increasing order; b itself is one of them, and for every listed block j the difference j // 2 - b // 2 is 0 or plus or minus a power of two of at most 8.
All inputs are finite; a program needn't handle non-finite values.
Results may differ from a plain program's by a relative error of at most 0.0065.
Values may be sent and summed in bfloat16 or wider, within the bound.
A program may use at most 128 MiB of HBM per device.

v0:
```python
import math

import jax
import jax.numpy as jnp
from jax import lax
from jax.sharding import PartitionSpec as P

DH = 128
BLOCK = 128
REACH = 8


very_negative = -1e30


def passed_along(value, axis, steps):
    count = lax.axis_size(axis)
    leading, last = (max(0, -steps), min(count, count - steps))
    return lax.ppermute(value, axis, [(source, source + steps) for source in range(leading, last)])


def padded(block, sides, width):
    for axis, dim in sides:
        count = lax.axis_size(axis)
        forward = [(i, i + 1) for i in range(count - 1)]
        backward = [(target, source) for source, target in forward]
        low = lax.ppermute(
            lax.slice_in_dim(block, block.shape[dim] - width, None, axis=dim), axis, forward
        )
        high = lax.ppermute(lax.slice_in_dim(block, 0, width, axis=dim), axis, backward)
        block = jnp.concatenate([low, block, high], axis=dim)
    return block


def tile_mask(kept_blocks, source_device, local_blocks):
    first_block = source_device * local_blocks
    block_ids = first_block + jnp.arange(local_blocks, dtype=jnp.int32)
    return jnp.any(kept_blocks[:, :, None] == block_ids[None, None, :], axis=1)


def absorb_block(running, query_rows, key_rows, value_rows, allowed_rows):
    running_top, denominator, numerator = running
    scores = jnp.einsum("qhd,khd->hqk", query_rows, key_rows, preferred_element_type=jnp.float32)
    scores = scores * (1.0 / math.sqrt(query_rows.shape[-1]))
    masked = jnp.where(allowed_rows[None], scores, very_negative)
    new_top = jnp.maximum(running_top, jnp.max(masked, axis=-1))
    weight = jnp.where(allowed_rows[None], jnp.exp(scores - new_top[..., None]), 0.0)
    rescale = jnp.exp(running_top - new_top)
    denominator = denominator * rescale + jnp.sum(weight, axis=-1)
    rounded = weight.astype(jnp.bfloat16)
    numerator = numerator * jnp.transpose(rescale)[:, :, None] + jnp.einsum(
        "hqk,khd->qhd", rounded, value_rows, preferred_element_type=jnp.float32
    )
    return (new_top, denominator, numerator)


def absorb_tile(states, key_tile, source_device, kept_blocks, query_blocks):
    local_blocks, block_len, heads, head_dim = query_blocks.shape
    key_rows = key_tile[0].reshape(local_blocks * block_len, heads, head_dim)
    value_rows = key_tile[1].reshape(local_blocks * block_len, heads, head_dim)
    allowed = tile_mask(kept_blocks, source_device, local_blocks)
    updated = []
    for query_slot in range(local_blocks):
        running = states[query_slot]
        token_allowed = jnp.repeat(allowed[query_slot], block_len)[None, :]
        running = absorb_block(
            running, query_blocks[query_slot], key_rows, value_rows, token_allowed
        )
        updated.append(running)
    return updated


def fetch_distant(stacked, offset_by):
    return passed_along(stacked, "blk", offset_by)


def per_device(queries, keys, values, kept_blocks):
    cycle_size = lax.axis_size("blk")
    position = lax.axis_index("blk")
    local_rows = queries.shape[0]
    local_blocks = local_rows // BLOCK
    heads = queries.shape[1] // DH
    query_blocks = queries.reshape(local_blocks, BLOCK, heads, DH)
    states = []
    for query_slot in range(local_blocks):
        states.append(
            (
                jnp.full((heads, BLOCK), very_negative, jnp.float32),
                jnp.zeros((heads, BLOCK), jnp.float32),
                jnp.zeros((BLOCK, heads, DH), jnp.float32),
            )
        )
    stacked = jnp.stack((keys, values))
    states = absorb_tile(states, stacked, position, kept_blocks, query_blocks)
    neighbours = padded(stacked, (("blk", 1),), local_rows)
    states = absorb_tile(
        states, neighbours[:, :local_rows], position - 1, kept_blocks, query_blocks
    )
    states = absorb_tile(
        states, neighbours[:, 2 * local_rows :], position + 1, kept_blocks, query_blocks
    )
    farthest = min(REACH, cycle_size - 1)
    distance = 2
    while distance <= farthest:
        for direction in (1, -1):
            key_tile = fetch_distant(stacked, -direction * distance)
            states = absorb_tile(
                states, key_tile, position + direction * distance, kept_blocks, query_blocks
            )
        distance = distance * 2
    outputs = []
    for query_slot in range(local_blocks):
        running_top, denominator, numerator = states[query_slot]
        outputs.append(numerator / jnp.transpose(denominator)[:, :, None])
    attended = jnp.concatenate(outputs, axis=0).reshape(local_rows, heads * DH)
    return attended.astype(jnp.bfloat16)


def solution(mesh):
    placed = (
        P(("clip", "blk"), None),
        P(("clip", "blk"), None),
        P(("clip", "blk"), None),
        P(("clip", "blk"), None),
    )
    return jax.shard_map(
        per_device, mesh=mesh, in_specs=placed, out_specs=P(("clip", "blk"), None), check_vma=False
    )
```

profile of v0, /device:TPU:19, one launch (start us, length us, event | category | flops | bytes accessed | tf_op | source)
XLA Modules:
  0.0 357.1 jit_solution(14420054263135990229)
XLA Ops:
  0.0 1.6 copy.107
  1.6 2.1 copy.104
  3.7 1.7 pad_maximum_fusion
  5.4 3.0 collective-permute-start.2
  8.5 3.1 collective-permute-start
  11.6 1.3 collective-permute-start.7
  12.9 7.9 %collective-permute-start.6 = (bf16[2,256,2560]{1,2,0:T(8,128)(2,1)}, bf16[2,256,2560]{1,2,0:T(8,128)(2,1)}, u32[]{:S(2)}, u32[]{:S(2)}) collective-permute-start(bf16[2,256,2560]{1,2,0:T(8,128)(2,1)} %pad_maximum_fusion), channel_id=1, source_target_pairs={{8,0},{9,1},{10,2},{11,3},{12,4},{13,5},{14,6},{15,7},{24,16},{25,... | collective-permute-start | bytes 7864328 | tf_op jit(solution)/shard_map/ppermute | solution.py:19
  20.8 4.6 %collective-permute-start.5 = (bf16[2,256,2560]{1,2,0:T(8,128)(2,1)}, bf16[2,256,2560]{1,2,0:T(8,128)(2,1)}, u32[]{:S(2)}, u32[]{:S(2)}) collective-permute-start(bf16[2,256,2560]{1,2,0:T(8,128)(2,1)} %pad_maximum_fusion), channel_id=1, source_target_pairs={{0,4},{1,5},{2,6},{3,7},{4,8},{5,9},{6,10},{7,11},{8,12},{9,13},{1... | collective-permute-start | bytes 7864328 | tf_op jit(solution)/shard_map/ppermute | solution.py:19
  26.9 2.2 fusion.192
  29.2 1.4 copy.251
  31.3 2.2 select_reduce_fusion.17
  33.5 2.1 select_reduce_fusion.8
  35.6 47.8 %collective-permute-done.2 = bf16[2,256,2560]{1,2,0:T(8,128)(2,1)} collective-permute-done((bf16[2,256,2560]{1,2,0:T(8,128)(2,1)}, bf16[2,256,2560]{1,2,0:T(8,128)(2,1)}, u32[]{:S(2)}, u32[]{:S(2)}) %collective-permute-start.2) | collective-permute-done | bytes 2621472 | tf_op jit(solution)/shard_map/ppermute | solution.py:19
  83.4 1.9 collective-permute-start.3
  85.3 1.9 fusion.189
  87.2 13.6 %collective-permute-done = bf16[2,256,2560]{1,2,0:T(8,128)(2,1)} collective-permute-done((bf16[2,256,2560]{1,2,0:T(8,128)(2,1)}, bf16[2,256,2560]{1,2,0:T(8,128)(2,1)}, u32[]{:S(2)}, u32[]{:S(2)}) %collective-permute-start) | collective-permute-done | bytes 2621472 | tf_op jit(solution)/shard_map/ppermute | solution.py:27
  100.9 25.0 %collective-permute-start.1 = (bf16[2,256,2560]{1,2,0:T(8,128)(2,1)}, bf16[2,256,2560]{1,2,0:T(8,128)(2,1)S(1)}, u32[]{:S(2)}, u32[]{:S(2)}) collective-permute-start(bf16[2,256,2560]{1,2,0:T(8,128)(2,1)} %pad_maximum_fusion), channel_id=1, source_target_pairs={{1,0},{2,1},{3,2},{4,3},{5,4},{6,5},{7,6},{8,7},{9,8},{10,9},{11,1... | collective-permute-start | bytes 7864328 | tf_op jit(solution)/shard_map/ppermute | solution.py:30
  125.9 3.0 fusion.191
  131.8 135.8 %collective-permute-done.3 = bf16[2,256,2560]{1,2,0:T(8,128)(2,1)S(1)} collective-permute-done((bf16[2,256,2560]{1,2,0:T(8,128)(2,1)}, bf16[2,256,2560]{1,2,0:T(8,128)(2,1)S(1)}, u32[]{:S(2)}, u32[]{:S(2)}) %collective-permute-start.3) | collective-permute-done | bytes 2621472 | tf_op jit(solution)/shard_map/ppermute | solution.py:19
  267.6 2.1 collective-permute-start.4
  269.7 1.2 fusion.188
  272.4 2.9 fusion.184
  275.4 1.2 fusion.190
  278.1 1.9 fusion.185
  280.0 2.2 select_reduce_fusion.9
  282.2 2.2 select_reduce_fusion
  285.9 2.9 fusion.186
  290.3 14.4 %collective-permute-done.4 = bf16[2,256,2560]{1,2,0:T(8,128)(2,1)S(1)} collective-permute-done((bf16[2,256,2560]{1,2,0:T(8,128)(2,1)}, bf16[2,256,2560]{1,2,0:T(8,128)(2,1)S(1)}, u32[]{:S(2)}, u32[]{:S(2)}) %collective-permute-start.4) | collective-permute-done | bytes 2621472 | tf_op jit(solution)/shard_map/ppermute | solution.py:19
  304.6 1.2 fusion.187
  321.3 4.0 %fusion.39 = f32[128,20,128]{2,0,1:T(8,128)} fusion(bf16[256,20,128]{0,2,1:T(8,128)(2,1)S(1)} %bitcast.656, f32[20,128,256]{2,1,0:T(8,128)} %get-tuple-element.127, f32[20,128]{1,0:T(8,128)S(1)} %get-tuple-element.71, pred[256]{0:T(512)(128)(4,1)S(1)} %get-tuple-element.137, f32[128,20]{0,1:T(8,128)S(1)} %get-tuple-element.68, ...), kind=kOutput, calls=%fused_computation.126 | convolution fusion | flops 171048960 | bytes 5273856 | tf_op jit(solution)/shard_map/hqk,khd->qhd/dot_general | solution.py:51
  325.4 4.6 %fusion.21 = f32[128,20,128]{2,0,1:T(8,128)} fusion(bf16[256,20,128]{0,2,1:T(8,128)(2,1)} %bitcast.655, f32[20,128,256]{2,1,0:T(8,128)} %get-tuple-element.109, f32[20,128]{1,0:T(8,128)S(1)} %get-tuple-element.73, pred[256]{0:T(512)(128)(4,1)S(1)} %get-tuple-element.136, f32[128,20]{0,1:T(8,128)S(1)} %get-tuple-element.69, f32[128,20]{0,1:T(8,128)S(1)} %get-tuple-element.72), kind=kOutput, calls=%fused_computation.99 | convolution fusion | flops 171048960 | bytes 5273856 | tf_op jit(solution)/shard_map/hqk,khd->qhd/dot_general | solution.py:51
  330.0 3.8 %fusion.37 = f32[128,20,128]{2,0,1:T(8,128)} fusion(f32[128,20,128]{2,0,1:T(8,128)} %fusion.39, bf16[256,20,128]{0,2,1:T(8,128)(2,1)S(1)} %bitcast.630, f32[20,256,128]{2,1,0:T(8,128)S(1)} %get-tuple-element.125, f32[20,128]{1,0:T(8,128)S(1)} %get-tuple-element.29, pred[256]{0:T(512)(128)(4,1)S(1)} %broadcast_bitcast_fusion.16, ...), kind=kOutput, calls=%fused_computation.123 | convolution fusion | flops 171048960 | bytes 6574336 | tf_op jit(solution)/shard_map/hqk,khd->qhd/dot_general | solution.py:51
  333.8 2.4 fusion.19
  336.2 2.3 fusion.35
  338.5 1.0 fusion.17
  339.5 1.0 fusion.33
  340.6 1.0 fusion.15
  341.9 1.0 fusion.31
  342.9 1.0 fusion.13
  344.2 1.0 fusion.29
  345.2 1.0 fusion.11
  346.5 1.0 fusion.27
  347.5 1.0 fusion.9
  348.5 1.2 fusion.25
  349.7 1.0 fusion.7
  351.8 1.1 fusion.40
  353.6 1.1 fusion.41
  355.4 1.6 copy.180
  (107 shorter events, 29.6 us)
Async XLA Ops:
  1.6 27.6 %copy-start.11 = (bf16[256,2560]{0,1:T(8,128)(2,1)}, bf16[256,2560]{0,1:T(8,128)(2,1)S(1)}, u32[]{:S(2)}) copy-start(bf16[256,2560]{0,1:T(8,128)(2,1)S(1)} %copy.107) | copy-start | bytes 3932164
  3.7 21.9 %copy-start.14 = (s32[2,8]{1,0:T(2,128)S(1)}, s32[2,8]{1,0:T(2,128)}, u32[]{:S(2)}) copy-start(s32[2,8]{1,0:T(2,128)} %param.7) | copy-start | bytes 196
  5.4 78.0 %collective-permute-start.2 = (bf16[2,256,2560]{1,2,0:T(8,128)(2,1)}, bf16[2,256,2560]{1,2,0:T(8,128)(2,1)}, u32[]{:S(2)}, u32[]{:S(2)}) collective-permute-start(bf16[2,256,2560]{1,2,0:T(8,128)(2,1)} %pad_maximum_fusion), channel_id=1, source_target_pairs={{2,0},{3,1},{4,2},{5,3},{6,4},{7,5},{8,6},{9,7},{10,8},{11,9},{12,... | collective-permute-start | bytes 7864328 | tf_op jit(solution)/shard_map/ppermute | solution.py:19
  8.5 92.4 %collective-permute-start = (bf16[2,256,2560]{1,2,0:T(8,128)(2,1)}, bf16[2,256,2560]{1,2,0:T(8,128)(2,1)}, u32[]{:S(2)}, u32[]{:S(2)}) collective-permute-start(bf16[2,256,2560]{1,2,0:T(8,128)(2,1)} %pad_maximum_fusion), channel_id=1, source_target_pairs={{0,1},{1,2},{2,3},{3,4},{4,5},{5,6},{6,7},{7,8},{8,9},{9,10},{10,1... | collective-permute-start | bytes 7864328 | tf_op jit(solution)/shard_map/ppermute | solution.py:27
  11.6 260.8 %collective-permute-start.7 = (bf16[2,256,2560]{1,2,0:T(8,128)(2,1)}, bf16[2,256,2560]{1,2,0:T(8,128)(2,1)}, u32[]{:S(2)}, u32[]{:S(2)}) collective-permute-start(bf16[2,256,2560]{1,2,0:T(8,128)(2,1)} %pad_maximum_fusion), channel_id=1, source_target_pairs={{0,8},{1,9},{2,10},{3,11},{4,12},{5,13},{6,14},{7,15},{16,24},{17,... | collective-permute-start | bytes 7864328 | tf_op jit(solution)/shard_map/ppermute | solution.py:19
  12.9 265.2 %collective-permute-start.6 = (bf16[2,256,2560]{1,2,0:T(8,128)(2,1)}, bf16[2,256,2560]{1,2,0:T(8,128)(2,1)}, u32[]{:S(2)}, u32[]{:S(2)}) collective-permute-start(bf16[2,256,2560]{1,2,0:T(8,128)(2,1)} %pad_maximum_fusion), channel_id=1, source_target_pairs={{8,0},{9,1},{10,2},{11,3},{12,4},{13,5},{14,6},{15,7},{24,16},{25,... | collective-permute-start | bytes 7864328 | tf_op jit(solution)/shard_map/ppermute | solution.py:19
  20.8 265.1 %collective-permute-start.5 = (bf16[2,256,2560]{1,2,0:T(8,128)(2,1)}, bf16[2,256,2560]{1,2,0:T(8,128)(2,1)}, u32[]{:S(2)}, u32[]{:S(2)}) collective-permute-start(bf16[2,256,2560]{1,2,0:T(8,128)(2,1)} %pad_maximum_fusion), channel_id=1, source_target_pairs={{0,4},{1,5},{2,6},{3,7},{4,8},{5,9},{6,10},{7,11},{8,12},{9,13},{1... | collective-permute-start | bytes 7864328 | tf_op jit(solution)/shard_map/ppermute | solution.py:19
  83.4 184.2 %collective-permute-start.3 = (bf16[2,256,2560]{1,2,0:T(8,128)(2,1)}, bf16[2,256,2560]{1,2,0:T(8,128)(2,1)S(1)}, u32[]{:S(2)}, u32[]{:S(2)}) collective-permute-start(bf16[2,256,2560]{1,2,0:T(8,128)(2,1)} %pad_maximum_fusion), channel_id=1, source_target_pairs={{0,2},{1,3},{2,4},{3,5},{4,6},{5,7},{6,8},{7,9},{8,10},{9,11},{10,... | collective-permute-start | bytes 7864328 | tf_op jit(solution)/shard_map/ppermute | solution.py:19
  100.9 174.5 %collective-permute-start.1 = (bf16[2,256,2560]{1,2,0:T(8,128)(2,1)}, bf16[2,256,2560]{1,2,0:T(8,128)(2,1)S(1)}, u32[]{:S(2)}, u32[]{:S(2)}) collective-permute-start(bf16[2,256,2560]{1,2,0:T(8,128)(2,1)} %pad_maximum_fusion), channel_id=1, source_target_pairs={{1,0},{2,1},{3,2},{4,3},{5,4},{6,5},{7,6},{8,7},{9,8},{10,9},{11,1... | collective-permute-start | bytes 7864328 | tf_op jit(solution)/shard_map/ppermute | solution.py:30
  267.6 37.0 %collective-permute-start.4 = (bf16[2,256,2560]{1,2,0:T(8,128)(2,1)}, bf16[2,256,2560]{1,2,0:T(8,128)(2,1)S(1)}, u32[]{:S(2)}, u32[]{:S(2)}) collective-permute-start(bf16[2,256,2560]{1,2,0:T(8,128)(2,1)} %pad_maximum_fusion), channel_id=1, source_target_pairs={{4,0},{5,1},{6,2},{7,3},{8,4},{9,5},{10,6},{11,7},{12,8},{13,9},{1... | collective-permute-start | bytes 7864328 | tf_op jit(solution)/shard_map/ppermute | solution.py:19
  306.6 1.7 copy-start.10
  312.4 1.7 copy-start.7
  313.0 2.1 copy-start.9
  318.9 1.7 copy-start.5
  319.5 1.8 copy-start.12
  325.4 4.6 %copy-start.1 = (bf16[1,256,2560]{1,2,0:T(8,128)(2,1)S(1)}, bf16[1,256,2560]{1,2,0:T(8,128)(2,1)}, u32[]{:S(2)}) copy-start(bf16[1,256,2560]{1,2,0:T(8,128)(2,1)} %get-tuple-element.64) | copy-start | bytes 3932164
  333.8 2.4 copy-start.3
  340.5 1.3 copy-start
  342.9 1.3 copy-start.4
  345.2 1.3 copy-start.2
  349.7 1.7 copy-start.8
  349.7 2.1 copy-start.13
  351.8 1.7 copy-start.6
where the time goes:
time: 364 us; the launch traced here: 357 us
  waiting for transfers between devices  212 us (58%)
  matrix products  49.5 us (14%)
  starting transfers between devices  49 us (13%)
  local copies, waits for them, and re-layouts  32.5 us (9%)
  other arithmetic  13.8 us (4%)
    ppermute x6, waiting for transfers between devices, passed_along(): lax.ppermute(value, axis, [(source, source + steps) for source in range(l...  198 us
    dot_general x18, matrix products, absorb_block(): jnp.einsum('hqk,khd->qhd', rounded, value_rows, preferred_element_type=jn...  30.5 us
    ppermute x1, starting transfers between devices, padded(): lax.ppermute(lax.slice_in_dim(block, 0, width, axis=dim), axis, backward)  25 us
    ppermute x6, starting transfers between devices, passed_along(): lax.ppermute(value, axis, [(source, source + steps) for source in range(l...  20.8 us
    dot_general x18, matrix products, absorb_block(): jnp.einsum('qhd,khd->hqk', query_rows, key_rows, preferred_element_type=j...  18.9 us
    slice x8, local copies, waits for them, and re-layouts, absorb_tile(): value_rows = key_tile[1].reshape(local_blocks * block_len, heads, head_dim)  16.3 us
    ppermute x1, waiting for transfers between devices, padded(): lax.ppermute(lax.slice_in_dim(block, block.shape[dim] - width, None, axis...  13.6 us
    reduce_sum x18, other arithmetic, absorb_block(): denominator = denominator * rescale + jnp.sum(weight, axis=-1)  11.3 us
  transfers between devices with their start and end apart: 8, of which 4 were waited for; matrix products, arithmetic and copies ran while one was open for 11% of the time, Pallas kernels for 0%

commit v1 on v0

v1 whole, which is shorter than its diff:
```python
import functools
import math

import jax
import jax.numpy as jnp
from jax import lax
from jax.experimental import pallas as pl
from jax.experimental.pallas import tpu as pltpu
from jax.sharding import PartitionSpec as P

DH = 128
BLOCK = 128
HEADS_PER_GROUP = 1
LEAD = 3

OFFSETS = (1, -1, 2, -2, 4, -4, 8, -8, 0)
OWN = 8
MASKED = -1e30
C_EXP = math.log2(math.e) / math.sqrt(DH)


def kernel(
    n, groups, kept_ref, q_hbm, k_hbm, v_hbm, out_ref,
    kv, q_vmem, scores, bias, local_sem, q_sem, send_sem, recv_sem,
):
    width = kv.shape[-1]
    rows = kv.shape[-2]
    local_blocks = rows // BLOCK
    d = lax.axis_index("blk")
    r = lax.rem(d, 4)
    upper = r // 2
    odd = lax.rem(r, 2)

    pair = d + 2 - 4 * upper
    mate = d + 1 - 2 * odd
    has_up = d + 4 < n
    has_down = d - 4 >= 0

    def columns(g):
        return pl.ds(pl.multiple_of(g * width, width), width)

    def local_copies(g):
        return [
            pltpu.make_async_copy(hbm.at[:, columns(g)], kv.at[OWN, g, i], local_sem.at[i, g])
            for i, hbm in ((0, k_hbm), (1, v_hbm))
        ]

    def flow(index, src_slot, dst_slot, target, g):
        return pltpu.make_async_remote_copy(
            src_ref=kv.at[src_slot, g],
            dst_ref=kv.at[dst_slot, g],
            send_sem=send_sem.at[index, g],
            recv_sem=recv_sem.at[dst_slot, g],
            device_id={"blk": target},
            device_id_type=pl.DeviceIdType.MESH,
        )

    def received(slot, sender, g):
        return pltpu.make_async_remote_copy(
            src_ref=kv.at[slot, g],
            dst_ref=kv.at[slot, g],
            send_sem=send_sem.at[0, g],
            recv_sem=recv_sem.at[slot, g],
            device_id={"blk": sender},
            device_id_type=pl.DeviceIdType.MESH,
        )

    own_flows = (
        (0, OWN, 5, d + 4, has_up),
        (1, OWN, 4, d - 4, has_down),
        (2, OWN, 3 - upper, pair, None),
        (3, OWN, 1 - odd, mate, None),
    )
    both = jnp.logical_and(has_up, has_down)
    pass_flows = (
        (4, 5, 7, d + 4, both),
        (5, 4, 6, d - 4, both),
        (6, 4 + upper, 2 + upper, pair, jnp.where(upper == 1, d - 4 >= 0, d + 4 < n)),
    )
    mate_flows = (
        (7, 2 + odd, odd, mate, jnp.where(odd == 1, d - 2 >= 0, d + 2 < n)),
    )

    def when(condition, action):
        if condition is None:
            action()
        else:
            pl.when(condition)(action)

    def start(flows, g):
        for index, src, dst, target, condition in flows:
            when(condition, lambda: flow(index, src, dst, target, g).start())

    def arrive(slot, sender, condition, g):
        when(condition, lambda: received(slot, sender, g).wait_recv())

    pl.loop(0, groups)(lambda g: [c.start() for c in local_copies(g)] and None)
    q_copy = pltpu.make_async_copy(q_hbm, q_vmem, q_sem)
    q_copy.start()

    barrier = pltpu.get_barrier_semaphore()
    for target, condition in ((d + 4, has_up), (d - 4, has_down), (pair, None), (mate, None)):
        when(
            condition,
            lambda: pl.semaphore_signal(
                barrier, inc=1, device_id={"blk": target}, device_id_type=pl.DeviceIdType.MESH
            ),
        )
    pl.semaphore_wait(barrier, 2 + has_up.astype(jnp.int32) + has_down.astype(jnp.int32))

    def send_own(g):
        for c in local_copies(g):
            c.wait()
        start(own_flows, g)

    for g in range(min(LEAD, groups)):
        send_own(g)

    for slot, offset in enumerate(OFFSETS[:OWN]):
        source = d + offset

        @pl.when(jnp.logical_or(source < 0, source >= n))
        def _():
            @pl.loop(0, groups)
            def _(g):
                kv[slot, g] = jnp.zeros(kv.shape[2:], kv.dtype)

    for query_slot in range(local_blocks):
        kept = [kept_ref[query_slot, j] for j in range(kept_ref.shape[1])]
        for slot, offset in enumerate(OFFSETS):
            for key_slot in range(local_blocks):
                block = (d + offset) * local_blocks + key_slot
                allowed = functools.reduce(jnp.logical_or, [j == block for j in kept])
                allowed = jnp.logical_and(allowed, jnp.logical_and(d + offset >= 0, d + offset < n))
                bias[pl.ds(query_slot, 1), pl.ds(slot * rows + key_slot * BLOCK, BLOCK)] = jnp.full(
                    (1, BLOCK), jnp.where(allowed, 0.0, MASKED), jnp.float32
                )
    q_copy.wait()

    def attend(g):
        for head in range(width // DH):
            lanes = pl.ds(head * DH, DH)
            q = q_vmem[:, pl.ds(pl.multiple_of(g * width + head * DH, DH), DH)]
            tops = [None] * local_blocks
            for slot in range(len(OFFSETS)):
                s = lax.dot_general(
                    q, kv[slot, g, 0, :, lanes], (((1,), (1,)), ((), ())),
                    preferred_element_type=jnp.float32,
                )
                for b in range(local_blocks):
                    part = s[b * BLOCK : (b + 1) * BLOCK] + bias[b : b + 1, slot * rows : (slot + 1) * rows]
                    scores[slot, b * BLOCK : (b + 1) * BLOCK] = part
                    tops[b] = part if tops[b] is None else jnp.maximum(tops[b], part)
            top = jnp.concatenate([jnp.max(t, axis=1, keepdims=True) for t in tops], axis=0)
            sums = None
            numerator = None
            for slot in range(len(OFFSETS)):
                weight = jnp.exp2((scores[slot] - top) * C_EXP)
                sums = weight if sums is None else sums + weight
                term = jnp.dot(
                    weight.astype(jnp.bfloat16), kv[slot, g, 1, :, lanes],
                    preferred_element_type=jnp.float32,
                )
                numerator = term if numerator is None else numerator + term
            total = jnp.sum(sums, axis=1, keepdims=True)
            out_ref[:, pl.ds(pl.multiple_of(g * width + head * DH, DH), DH)] = (
                numerator / total
            ).astype(out_ref.dtype)

    @pl.loop(0, groups + 2)
    def _(t):
        @pl.when(t + LEAD < groups)
        def _():
            send_own(t + LEAD)

        @pl.when(t < groups)
        def _():
            arrive(5, d - 4, has_down, t)
            arrive(4, d + 4, has_up, t)
            start(pass_flows, t)

        @pl.when(jnp.logical_and(t >= 1, t < groups + 1))
        def _():
            g = t - 1
            arrive(2 + upper, pair, None, g)
            arrive(3 - upper, pair, jnp.where(upper == 1, d + 2 < n, d - 2 >= 0), g)
            start(mate_flows, g)

        @pl.when(t >= 2)
        def _():
            g = t - 2
            arrive(odd, mate, None, g)
            arrive(1 - odd, mate, jnp.where(odd == 1, d + 1 < n, d - 1 >= 0), g)
            arrive(7, d - 4, d - 8 >= 0, g)
            arrive(6, d + 4, d + 8 < n, g)
            attend(g)

    @pl.loop(0, groups)
    def _(g):
        for index, src, dst, target, condition in own_flows + pass_flows + mate_flows:
            when(condition, lambda: flow(index, src, dst, target, g).wait_send())


def per_device(queries, keys, values, kept_blocks):
    n = lax.axis_size("blk")
    rows, features = queries.shape
    width = HEADS_PER_GROUP * DH
    groups = features // width
    slots = len(OFFSETS)
    return pl.pallas_call(
        functools.partial(kernel, n, groups),
        out_shape=jax.ShapeDtypeStruct((rows, features), jnp.bfloat16),
        in_specs=[pl.BlockSpec(memory_space=pltpu.SMEM)] + [pl.BlockSpec(memory_space=pl.ANY)] * 3,
        out_specs=pl.BlockSpec(memory_space=pltpu.VMEM),
        scratch_shapes=[
            pltpu.VMEM((slots, groups, 2, rows, width), jnp.bfloat16),
            pltpu.VMEM((rows, features), jnp.bfloat16),
            pltpu.VMEM((slots, rows, rows), jnp.float32),
            pltpu.VMEM((rows // BLOCK, slots * rows), jnp.float32),
            pltpu.SemaphoreType.DMA((2, groups)),
            pltpu.SemaphoreType.DMA,
            pltpu.SemaphoreType.DMA((8, groups)),
            pltpu.SemaphoreType.DMA((8, groups)),
        ],
        compiler_params=pltpu.CompilerParams(
            collective_id=0, has_side_effects=True, vmem_limit_bytes=48 * 2**20
        ),
    )(kept_blocks, queries, keys, values)


def solution(mesh):
    placed = P(("clip", "blk"), None)
    return jax.shard_map(
        per_device, mesh=mesh, in_specs=(placed,) * 4, out_specs=placed, check_vma=False
    )
```

time: 364 us -> 131 us (0.36); the launches traced: 357 us -> 130 us
  waiting for transfers between devices: 212 us -> 0 us
  Pallas kernels: 0 us -> 124 us
  matrix products: 49.5 us -> 0 us
  starting transfers between devices: 49 us -> 0 us
  local copies, waits for them, and re-layouts: 32.5 us -> 5.68 us
  other arithmetic: 13.8 us -> 0 us
    ppermute x8 -> x0, waiting for transfers between devices: 212 us -> none  [the longest x6 198 us: passed_along(): lax.ppermute(value, axis, [(source, source + steps) for source in range(l...]
    pallas_call x0 -> x1, Pallas kernels: none -> 124 us  [per_device(): pl.pallas_call(functools.partial(kernel, n, groups), out_shape=jax.ShapeD...]
    dot_general x36 -> x0, matrix products: 49.5 us -> none  [the longest x18 30.5 us: absorb_block(): jnp.einsum('hqk,khd->qhd', rounded, value_rows, preferred_element_type=jn...]
    ppermute x8 -> x0, starting transfers between devices: 49 us -> none  [the longest x1 25 us: padded(): lax.ppermute(lax.slice_in_dim(block, 0, width, axis=dim), axis, backward)]
    slice x9 -> x0, local copies, waits for them, and re-layouts: 18.5 us -> none  [the longest x8 16.3 us: absorb_tile(): value_rows = key_tile[1].reshape(local_blocks * block_len, heads, head_dim)]
    reduce_sum x18 -> x0, other arithmetic: 11.3 us -> none  [absorb_block(): denominator = denominator * rescale + jnp.sum(weight, axis=-1)]
    unnamed x34 -> x9, local copies, waits for them, and re-layouts: 10.5 us -> 5.68 us
  transfers between devices with their start and end apart: 8 -> 0, of which waited for: 4 -> 0; matrix products, arithmetic and copies ran while one was open for 11% -> 0% of each run, Pallas kernels for 0% -> 0%
where the time goes in v1:
time: 131 us; the launch traced here: 130 us
  Pallas kernels  124 us (95%)
  local copies, waits for them, and re-layouts  5.68 us (4%)
    pallas_call x1, Pallas kernels, per_device(): pl.pallas_call(functools.partial(kernel, n, groups), out_shape=jax.ShapeD...  124 us
    unnamed x9, local copies, waits for them, and re-layouts  5.68 us

profile of v1, /device:TPU:19, one launch (start us, length us, event | category | flops | bytes accessed | tf_op | source)
XLA Modules:
  0.0 130.0 jit_solution(4766881778534462869)
XLA Ops:
  0.0 0.0 copy-start
  0.0 1.3 %copy-done = bf16[256,2560]{1,0:T(8,128)(2,1)S(1)} copy-done((bf16[256,2560]{1,0:T(8,128)(2,1)S(1)}, bf16[256,2560]{1,0:T(8,128)(2,1)}, u32[]{:S(2)}) %copy-start) | copy-done | bytes 1310744
  1.3 0.0 copy-start.1
  1.3 1.3 %copy-done.1 = bf16[256,2560]{1,0:T(8,128)(2,1)S(1)} copy-done((bf16[256,2560]{1,0:T(8,128)(2,1)S(1)}, bf16[256,2560]{1,0:T(8,128)(2,1)}, u32[]{:S(2)}) %copy-start.1) | copy-done | bytes 1310744
  2.6 0.0 copy-start.2
  2.6 1.3 %copy-done.2 = bf16[256,2560]{1,0:T(8,128)(2,1)S(1)} copy-done((bf16[256,2560]{1,0:T(8,128)(2,1)S(1)}, bf16[256,2560]{1,0:T(8,128)(2,1)}, u32[]{:S(2)}) %copy-start.2) | copy-done | bytes 1310744
  4.0 0.0 copy-start.3
  4.0 0.7 copy-done.3
  4.6 124.3 %shard_map.46 = bf16[256,2560]{1,0:T(8,128)(2,1)S(1)} custom-call(s32[2,8]{1,0:T(2,128)S(1)} %copy-done.3, bf16[256,2560]{1,0:T(8,128)(2,1)S(1)} %copy-done, bf16[256,2560]{1,0:T(8,128)(2,1)S(1)} %copy-done.1, bf16[256,2560]{1,0:T(8,128)(2,1)S(1)} %copy-done.2), custom_call_target="tpu_custom_call" | custom-call | tf_op jit(solution)/shard_map/pallas_call | solution.py:210
  129.0 1.1 copy.6
Async XLA Ops:
  0.0 1.3 %copy-start = (bf16[256,2560]{1,0:T(8,128)(2,1)S(1)}, bf16[256,2560]{1,0:T(8,128)(2,1)}, u32[]{:S(2)}) copy-start(bf16[256,2560]{1,0:T(8,128)(2,1)} %q_hbm.1) | copy-start | bytes 3932164
  1.3 1.3 %copy-start.1 = (bf16[256,2560]{1,0:T(8,128)(2,1)S(1)}, bf16[256,2560]{1,0:T(8,128)(2,1)}, u32[]{:S(2)}) copy-start(bf16[256,2560]{1,0:T(8,128)(2,1)} %k_hbm.1) | copy-start | bytes 3932164
  2.6 1.3 %copy-start.2 = (bf16[256,2560]{1,0:T(8,128)(2,1)S(1)}, bf16[256,2560]{1,0:T(8,128)(2,1)}, u32[]{:S(2)}) copy-start(bf16[256,2560]{1,0:T(8,128)(2,1)} %v_hbm.1) | copy-start | bytes 3932164
  4.0 0.7 copy-start.3

commit v2 on v1

--- a/solution.py
+++ b/solution.py
@@ -11,7 +11,7 @@
 DH = 128
 BLOCK = 128
 HEADS_PER_GROUP = 1
-LEAD = 3
+LEAD = 1
 
 OFFSETS = (1, -1, 2, -2, 4, -4, 8, -8, 0)
 OWN = 8
@@ -20,8 +20,8 @@
 
 
 def kernel(
-    n, groups, kept_ref, q_hbm, k_hbm, v_hbm, out_ref,
-    kv, q_vmem, scores, bias, local_sem, q_sem, send_sem, recv_sem,
+    n, groups, kept_hbm, q_hbm, k_hbm, v_hbm, out_hbm,
+    kv, kept_ref, q_vmem, scores, bias, out_ref, local_sem, kept_sem, q_sem, out_sem, send_sem, recv_sem,
 ):
     width = kv.shape[-1]
     rows = kv.shape[-2]
@@ -94,10 +94,6 @@
     def arrive(slot, sender, condition, g):
         when(condition, lambda: received(slot, sender, g).wait_recv())
 
-    pl.loop(0, groups)(lambda g: [c.start() for c in local_copies(g)] and None)
-    q_copy = pltpu.make_async_copy(q_hbm, q_vmem, q_sem)
-    q_copy.start()
-
     barrier = pltpu.get_barrier_semaphore()
     for target, condition in ((d + 4, has_up), (d - 4, has_down), (pair, None), (mate, None)):
         when(
@@ -106,6 +102,16 @@
                 barrier, inc=1, device_id={"blk": target}, device_id_type=pl.DeviceIdType.MESH
             ),
         )
+
+    @pl.loop(0, groups)
+    def _(g):
+        for c in local_copies(g):
+            c.start()
+
+    q_copy = pltpu.make_async_copy(q_hbm, q_vmem, q_sem)
+    q_copy.start()
+    kept_copy = pltpu.make_async_copy(kept_hbm, kept_ref, kept_sem)
+    kept_copy.start()
     pl.semaphore_wait(barrier, 2 + has_up.astype(jnp.int32) + has_down.astype(jnp.int32))
 
     def send_own(g):
@@ -125,6 +131,7 @@
             def _(g):
                 kv[slot, g] = jnp.zeros(kv.shape[2:], kv.dtype)
 
+    kept_copy.wait()
     for query_slot in range(local_blocks):
         kept = [kept_ref[query_slot, j] for j in range(kept_ref.shape[1])]
         for slot, offset in enumerate(OFFSETS):
@@ -136,6 +143,11 @@
                     (1, BLOCK), jnp.where(allowed, 0.0, MASKED), jnp.float32
                 )
     q_copy.wait()
+
+    def out_copy(g):
+        return pltpu.make_async_copy(
+            out_ref.at[:, columns(g)], out_hbm.at[:, columns(g)], out_sem.at[g]
+        )
 
     def attend(g):
         for head in range(width // DH):
@@ -166,6 +178,7 @@
             out_ref[:, pl.ds(pl.multiple_of(g * width + head * DH, DH), DH)] = (
                 numerator / total
             ).astype(out_ref.dtype)
+        out_copy(g).start()
 
     @pl.loop(0, groups + 2)
     def _(t):
@@ -199,6 +212,7 @@
     def _(g):
         for index, src, dst, target, condition in own_flows + pass_flows + mate_flows:
             when(condition, lambda: flow(index, src, dst, target, g).wait_send())
+        out_copy(g).wait()
 
 
 def per_device(queries, keys, values, kept_blocks):
@@ -210,20 +224,24 @@
     return pl.pallas_call(
         functools.partial(kernel, n, groups),
         out_shape=jax.ShapeDtypeStruct((rows, features), jnp.bfloat16),
-        in_specs=[pl.BlockSpec(memory_space=pltpu.SMEM)] + [pl.BlockSpec(memory_space=pl.ANY)] * 3,
-        out_specs=pl.BlockSpec(memory_space=pltpu.VMEM),
+        in_specs=[pl.BlockSpec(memory_space=pltpu.HBM)] * 4,
+        out_specs=pl.BlockSpec(memory_space=pltpu.HBM),
         scratch_shapes=[
             pltpu.VMEM((slots, groups, 2, rows, width), jnp.bfloat16),
+            pltpu.SMEM(kept_blocks.shape, jnp.int32),
             pltpu.VMEM((rows, features), jnp.bfloat16),
             pltpu.VMEM((slots, rows, rows), jnp.float32),
             pltpu.VMEM((rows // BLOCK, slots * rows), jnp.float32),
+            pltpu.VMEM((rows, features), jnp.bfloat16),
             pltpu.SemaphoreType.DMA((2, groups)),
             pltpu.SemaphoreType.DMA,
+            pltpu.SemaphoreType.DMA,
+            pltpu.SemaphoreType.DMA((groups,)),
             pltpu.SemaphoreType.DMA((8, groups)),
             pltpu.SemaphoreType.DMA((8, groups)),
         ],
         compiler_params=pltpu.CompilerParams(
-            collective_id=0, has_side_effects=True, vmem_limit_bytes=48 * 2**20
+            collective_id=0, has_side_effects=True, vmem_limit_bytes=67_043_328
         ),
     )(kept_blocks, queries, keys, values)
 

time: 131 us -> 126 us (0.962)
  local copies, waits for them, and re-layouts: 5.68 us -> 2.46 us
    unnamed x9 -> x1, local copies, waits for them, and re-layouts: 5.68 us -> 2.46 us
    pallas_call x1, Pallas kernels: 124 us -> 123 us  [per_device(): pl.pallas_call(functools.partial(kernel, n, groups), out_shape=jax.ShapeD...]
where the time goes in v2:
time: 126 us; the launch traced here: 125 us
  Pallas kernels  123 us (98%)
  local copies, waits for them, and re-layouts  2.46 us (2%)
    pallas_call x1, Pallas kernels, per_device(): pl.pallas_call(functools.partial(kernel, n, groups), out_shape=jax.ShapeD...  123 us

profile of v2, /device:TPU:19, one launch (start us, length us, event | category | flops | bytes accessed | tf_op | source)
XLA Modules:
  0.0 125.3 jit_solution(18425750459723756313)
XLA Ops:
  0.0 122.9 %shard_map.46 = bf16[256,2560]{1,0:T(8,128)(2,1)} custom-call(s32[2,8]{1,0:T(2,128)} %kept_hbm.1, bf16[256,2560]{1,0:T(8,128)(2,1)} %q_hbm.1, bf16[256,2560]{1,0:T(8,128)(2,1)} %k_hbm.1, bf16[256,2560]{1,0:T(8,128)(2,1)} %v_hbm.1), custom_call_target="tpu_custom_call" | custom-call | tf_op jit(solution)/shard_map/pallas_call | solution.py:224
  122.9 2.5 %copy.6 = bf16[256,2560]{1,0:T(8,128)(2,1)} copy(bf16[256,2560]{1,0:T(8,128)(2,1)} %shard_map.46) | data formatting | bytes 2621440

commit v3 on v2

v3 whole, which is shorter than its diff:
```python
import functools
import math

import jax
import jax.numpy as jnp
from jax import lax
from jax.experimental import pallas as pl
from jax.experimental.pallas import tpu as pltpu
from jax.sharding import PartitionSpec as P

DH = 128
BLOCK = 128
SINGLES = 4
LEAD = 1

OFFSETS = (1, -1, 2, -2, 4, -4, 8, -8, 0)
OWN = 8
MASKED = -1e30
C_EXP = math.log2(math.e) / math.sqrt(DH)


def kernel(
    n, heads, doubles, kept_hbm, q_hbm, k_hbm, v_hbm, out_hbm,
    kv, kept_ref, q_vmem, scores, bias, out_vmem, local_sem, kept_sem, q_sem, out_sem, send_sem, recv_sem,
):
    groups = heads - doubles
    rows = kv.shape[-2]
    local_blocks = rows // BLOCK
    d = lax.axis_index("blk")
    r = lax.rem(d, 4)
    upper = r // 2
    odd = lax.rem(r, 2)

    pair = d + 2 - 4 * upper
    mate = d + 1 - 2 * odd
    has_up = d + 4 < n
    has_down = d - 4 >= 0

    def columns(h):
        return pl.ds(pl.multiple_of(h * DH, DH), DH)

    def by_size(g, action):
        @pl.when(g < doubles)
        def _():
            action(g * 2, 2)

        @pl.when(g >= doubles)
        def _():
            action(g + doubles, 1)

    def local_copies(h):
        return [
            pltpu.make_async_copy(hbm.at[:, columns(h)], kv.at[OWN, h, i], local_sem.at[i, h])
            for i, hbm in ((0, k_hbm), (1, v_hbm))
        ]

    def flow(index, src_slot, dst_slot, target, g, first, size):
        return pltpu.make_async_remote_copy(
            src_ref=kv.at[src_slot, pl.ds(first, size)],
            dst_ref=kv.at[dst_slot, pl.ds(first, size)],
            send_sem=send_sem.at[index, g],
            recv_sem=recv_sem.at[dst_slot, g],
            device_id={"blk": target},
            device_id_type=pl.DeviceIdType.MESH,
        )

    def received(slot, sender, g, first, size):
        return pltpu.make_async_remote_copy(
            src_ref=kv.at[slot, pl.ds(first, size)],
            dst_ref=kv.at[slot, pl.ds(first, size)],
            send_sem=send_sem.at[0, g],
            recv_sem=recv_sem.at[slot, g],
            device_id={"blk": sender},
            device_id_type=pl.DeviceIdType.MESH,
        )

    own_flows = (
        (0, OWN, 5, d + 4, has_up),
        (1, OWN, 4, d - 4, has_down),
        (2, OWN, 3 - upper, pair, None),
        (3, OWN, 1 - odd, mate, None),
    )
    both = jnp.logical_and(has_up, has_down)
    pass_flows = (
        (4, 5, 7, d + 4, both),
        (5, 4, 6, d - 4, both),
        (6, 4 + upper, 2 + upper, pair, jnp.where(upper == 1, d - 4 >= 0, d + 4 < n)),
    )
    mate_flows = (
        (7, 2 + odd, odd, mate, jnp.where(odd == 1, d - 2 >= 0, d + 2 < n)),
    )

    def when(condition, action):
        if condition is None:
            action()
        else:
            pl.when(condition)(action)

    def start(flows, *chunk):
        for index, src, dst, target, condition in flows:
            when(condition, lambda: flow(index, src, dst, target, *chunk).start())

    def arrive(slot, sender, condition, *chunk):
        when(condition, lambda: received(slot, sender, *chunk).wait_recv())

    barrier = pltpu.get_barrier_semaphore()
    for target, condition in ((d + 4, has_up), (d - 4, has_down), (pair, None), (mate, None)):
        when(
            condition,
            lambda: pl.semaphore_signal(
                barrier, inc=1, device_id={"blk": target}, device_id_type=pl.DeviceIdType.MESH
            ),
        )

    @pl.loop(0, heads)
    def _(h):
        for c in local_copies(h):
            c.start()

    q_copy = pltpu.make_async_copy(q_hbm, q_vmem, q_sem)
    q_copy.start()
    kept_copy = pltpu.make_async_copy(kept_hbm, kept_ref, kept_sem)
    kept_copy.start()
    pl.semaphore_wait(barrier, 2 + has_up.astype(jnp.int32) + has_down.astype(jnp.int32))

    def send_own(g):
        def action(first, size):
            for h in range(size):
                for c in local_copies(first + h):
                    c.wait()
            start(own_flows, g, first, size)

        by_size(g, action)

    def clear(first, size):
        for slot, offset in enumerate(OFFSETS[:OWN]):
            source = d + offset

            @pl.when(jnp.logical_or(source < 0, source >= n))
            def _():
                for h in range(size):
                    kv[slot, first + h] = jnp.zeros(kv.shape[2:], kv.dtype)

    def prepare():
        kept_copy.wait()
        for query_slot in range(local_blocks):
            kept = [kept_ref[query_slot, j] for j in range(kept_ref.shape[1])]
            for slot, offset in enumerate(OFFSETS):
                inside = jnp.logical_and(d + offset >= 0, d + offset < n)
                for key_slot in range(local_blocks):
                    block = (d + offset) * local_blocks + key_slot
                    allowed = functools.reduce(jnp.logical_or, [j == block for j in kept])
                    bias[pl.ds(query_slot, 1), pl.ds(slot * rows + key_slot * BLOCK, BLOCK)] = jnp.full(
                        (1, BLOCK), jnp.where(jnp.logical_and(allowed, inside), 0.0, MASKED), jnp.float32
                    )
        q_copy.wait()

    for g in range(min(LEAD, groups)):
        send_own(jnp.int32(g))

    def out_copy(h):
        return pltpu.make_async_copy(
            out_vmem.at[:, columns(h)], out_hbm.at[:, columns(h)], out_sem.at[h]
        )

    def attend(h, arrivals):
        q = q_vmem[:, columns(h)]
        tops = [None] * local_blocks
        for step, slot in enumerate((8, 2, 3, 4, 5, 0, 1, 6, 7)):
            if step == 5:
                arrivals()
            s = lax.dot_general(
                q, kv[slot, h, 0], (((1,), (1,)), ((), ())), preferred_element_type=jnp.float32
            )
            for b in range(local_blocks):
                part = s[b * BLOCK : (b + 1) * BLOCK] + bias[b : b + 1, slot * rows : (slot + 1) * rows]
                scores[slot, b * BLOCK : (b + 1) * BLOCK] = part
                tops[b] = part if tops[b] is None else jnp.maximum(tops[b], part)
        top = jnp.concatenate([jnp.max(t, axis=1, keepdims=True) for t in tops], axis=0)
        sums = None
        numerator = None
        for slot in range(len(OFFSETS)):
            weight = jnp.exp2((scores[slot] - top) * C_EXP)
            sums = weight if sums is None else sums + weight
            term = jnp.dot(
                weight.astype(jnp.bfloat16), kv[slot, h, 1], preferred_element_type=jnp.float32
            )
            numerator = term if numerator is None else numerator + term
        total = jnp.sum(sums, axis=1, keepdims=True)
        out_vmem[:, columns(h)] = numerator / total
        out_copy(h).start()

    @pl.loop(0, groups + 2)
    def _(t):
        @pl.when(t + LEAD < groups)
        def _():
            send_own(t + LEAD)

        @pl.when(t < groups)
        def _():
            def action(first, size):
                clear(first, size)
                arrive(5, d - 4, has_down, t, first, size)
                arrive(4, d + 4, has_up, t, first, size)
                start(pass_flows, t, first, size)

            by_size(t, action)

        @pl.when(t == 0)
        def _():
            prepare()

        @pl.when(jnp.logical_and(t >= 1, t < groups + 1))
        def _():
            g = t - 1

            def action(*chunk):
                arrive(2 + upper, pair, None, g, *chunk)
                arrive(3 - upper, pair, jnp.where(upper == 1, d + 2 < n, d - 2 >= 0), g, *chunk)
                start(mate_flows, g, *chunk)

            by_size(g, action)

        @pl.when(t >= 2)
        def _():
            g = t - 2

            def action(first, size):
                def arrivals():
                    arrive(odd, mate, None, g, first, size)
                    arrive(1 - odd, mate, jnp.where(odd == 1, d + 1 < n, d - 1 >= 0), g, first, size)
                    arrive(7, d - 4, d - 8 >= 0, g, first, size)
                    arrive(6, d + 4, d + 8 < n, g, first, size)

                for h in range(size):
                    attend(first + h, arrivals if h == 0 else lambda: None)

            by_size(g, action)

    @pl.loop(0, groups)
    def _(g):
        def action(first, size):
            for index, src, dst, target, condition in own_flows + pass_flows + mate_flows:
                when(condition, lambda: flow(index, src, dst, target, g, first, size).wait_send())
            for h in range(size):
                out_copy(first + h).wait()

        by_size(g, action)


def per_device(queries, keys, values, kept_blocks):
    n = lax.axis_size("blk")
    rows, features = queries.shape
    heads = features // DH
    doubles = max(heads - SINGLES, 0) // 2
    groups = heads - doubles
    slots = len(OFFSETS)
    attended = pl.pallas_call(
        functools.partial(kernel, n, heads, doubles),
        out_shape=jax.ShapeDtypeStruct((rows, features), jnp.float32),
        in_specs=[pl.BlockSpec(memory_space=pltpu.HBM)] * 4,
        out_specs=pl.BlockSpec(memory_space=pltpu.HBM),
        scratch_shapes=[
            pltpu.VMEM((slots, heads, 2, rows, DH), jnp.bfloat16),
            pltpu.SMEM(kept_blocks.shape, jnp.int32),
            pltpu.VMEM((rows, features), jnp.bfloat16),
            pltpu.VMEM((slots, rows, rows), jnp.float32),
            pltpu.VMEM((rows // BLOCK, slots * rows), jnp.float32),
            pltpu.VMEM((rows, features), jnp.float32),
            pltpu.SemaphoreType.DMA((2, heads)),
            pltpu.SemaphoreType.DMA,
            pltpu.SemaphoreType.DMA,
            pltpu.SemaphoreType.DMA((heads,)),
            pltpu.SemaphoreType.DMA((8, groups)),
            pltpu.SemaphoreType.DMA((8, groups)),
        ],
        compiler_params=pltpu.CompilerParams(
            collective_id=0, has_side_effects=True, vmem_limit_bytes=67_043_328
        ),
    )(kept_blocks, queries, keys, values)
    return attended.astype(jnp.bfloat16)


def solution(mesh):
    placed = P(("clip", "blk"), None)
    return jax.shard_map(
        per_device, mesh=mesh, in_specs=(placed,) * 4, out_specs=placed, check_vma=False
    )
```

time: 126 us -> 125 us (level)
  other arithmetic: 0 us -> 2.93 us
  local copies, waits for them, and re-layouts: 2.46 us -> 0 us
  Pallas kernels: 123 us -> 121 us
    convert_element_type x0 -> x1, other arithmetic: none -> 2.93 us  [per_device(): return attended.astype(jnp.bfloat16)]
    unnamed x1 -> x0, local copies, waits for them, and re-layouts: 2.46 us -> none
    pallas_call x1, Pallas kernels: 123 us -> 121 us  [per_device(): pl.pallas_call(functools.partial(kernel, n, heads, doubles), out_shape=ja...]
where the time goes in v3:
time: 125 us; the launch traced here: 124 us
  Pallas kernels  121 us (97%)
  other arithmetic  2.93 us (2%)
    pallas_call x1, Pallas kernels, per_device(): pl.pallas_call(functools.partial(kernel, n, heads, doubles), out_shape=ja...  121 us
    convert_element_type x1, other arithmetic, per_device(): return attended.astype(jnp.bfloat16)  2.93 us

profile of v3, /device:TPU:19, one launch (start us, length us, event | category | flops | bytes accessed | tf_op | source)
XLA Modules:
  0.0 124.4 jit_solution(9119397304306544396)
XLA Ops:
  0.0 121.5 %shard_map.46 = f32[256,2560]{1,0:T(8,128)} custom-call(s32[2,8]{1,0:T(2,128)} %kept_hbm.1, bf16[256,2560]{1,0:T(8,128)(2,1)} %q_hbm.1, bf16[256,2560]{1,0:T(8,128)(2,1)} %k_hbm.1, bf16[256,2560]{1,0:T(8,128)(2,1)} %v_hbm.1), custom_call_target="tpu_custom_call" | custom-call | tf_op jit(solution)/shard_map/pallas_call | solution.py:258
  121.5 2.9 %convert_element_type.3 = bf16[256,2560]{1,0:T(8,128)(2,1)} convert(f32[256,2560]{1,0:T(8,128)} %shard_map.46) | non-fusion elementwise | flops 655360 | bytes 3932160 | tf_op jit(solution)/shard_map/convert_element_type | solution.py:281
